TPU v7x, 256 devices: a whole 4x4x8 slice. The times are simulated.
256 devices in a mesh: req: 64 (over z, x, core), tp: 4 (over y).
Axes of the slice: x: 4, y: 4, z: 8, core: 2. Of those that a mesh axis runs over, the one named last changes fastest.
Arguments:
- tokens_new: bfloat16 [64, 16, 2, 1024], P('req'), may hold values from -6 to 6
- prefix_len: int32 [64], replicated, may hold values from 1 to 4096, as said below
- tail_len: int32 [64, 16], P('req'), may hold values from 1 to 512, as said below
- pool_home: int32 [2048], replicated, may hold values from 0 to 63, as said below
- pool_page: int32 [2048], replicated, may hold values from 0 to 31
- slot_page_cache: bfloat16 [2048, 128, 2, 512], P('req', None, None, 'tp'), may hold values from -64 to 64
- tail_cache: bfloat16 [64, 16, 512, 2, 512], P('req', None, None, None, 'tp'), may hold values from -6 to 6
- routes: int32 [64, 16, 2, 8], P('req'), may hold values from 0 to 31, all different within a row; in each aligned block of 32 rows (0 to 31, 32 to 63, ..., all dimensions but the last counted through in order) at most 12 rows name the same one
- norm_gains: float32 [3, 1024], replicated, may hold values from 0.1 to 1.9
- query_weight: bfloat16 [1024, 1024], P(None, 'tp'), may hold values from -0.1875 to 0.1875
- key_value_weight: bfloat16 [1024, 2, 512], P(None, None, 'tp'), may hold values from -0.1875 to 0.1875
- out_weight: bfloat16 [1024, 1024], P('tp'), may hold values from -0.1875 to 0.1875
- router: bfloat16 [1024, 32], replicated, may hold values from -0.375 to 0.375
- expert_in: bfloat16 [64, 1024, 2, 512], P('req', None, None, 'tp'), as said below
- expert_out: bfloat16 [64, 512, 1024], P('req', 'tp'), as said below
- score_weight: float32 [1024], replicated, may hold values from -0.1875 to 0.1875
Outputs:
- layer_out: bfloat16 [64, 16, 2, 1024], P('req')
- row_score: float32 [64, 16, 2], P('req')
Inputs may be any that keep to these rules, and one draw needn't show every extreme that they name: `prefix_len`: some request has exactly 4096 prefix positions. `tail_len`: some sample has exactly 512 tail positions. `pool_home`: entry s * 32 + v describes slot v of the pool of device s of req. Every page 0 to 31 of every request lies in exactly one slot, and one device's pool holds either exactly 1 pages of a request or none of them. `routes`: in the 32 rows of one device no expert is named more than 12 times. `expert_in`: expert table copy c equals copy c mod 32. `expert_out`: expert table copy c equals copy c mod 32.
All inputs are finite; a program needn't handle non-finite values.
Results may differ from a plain program's by a relative error of at most 0.017.
Values may be sent and summed in bfloat16 or wider, within the bound.
A program may use at most 128 MiB of HBM per device.

v0:
```python
import jax
import jax.numpy as jnp
from jax import lax
from jax.sharding import PartitionSpec as P

HEAD_DIM = 64
MOST = 12
EPSILON = 1e-05
ROPE_BASE = 10000.0
LOWEST = -1e30


def rms_scale(values, gain_row):
    widened = values.astype(jnp.float32)
    return (
        widened
        * lax.rsqrt(jnp.mean(widened * widened, axis=-1, keepdims=True) + EPSILON)
        * gain_row
    )


def apply_rotary(vectors, token_positions):
    half_width = vectors.shape[-1] // 2
    frequency = ROPE_BASE ** (-jnp.arange(half_width, dtype=jnp.float32) / half_width)
    angles = token_positions.astype(jnp.float32)[..., None] * frequency
    cosine = jnp.cos(angles)[..., None, :]
    sine_part = jnp.sin(angles)[..., None, :]
    leading = vectors[..., :half_width]
    trailing = vectors[..., half_width:]
    return jnp.concatenate(
        [leading * cosine - trailing * sine_part, trailing * cosine + leading * sine_part], axis=-1
    )


def block_stats(scores, visible):
    block_top = jnp.max(jnp.where(visible, scores, LOWEST), axis=-1)
    weights = jnp.where(
        visible, jnp.exp(jnp.where(visible, scores - block_top[..., None], 0.0)), 0.0
    )
    return (block_top, jnp.sum(weights, axis=-1), weights.astype(jnp.bfloat16))


def shards(
    tokens_new,
    prefix_len,
    tail_len,
    pool_home,
    pool_page,
    slot_page_cache,
    tail_cache,
    routes,
    norm_gains,
    query_weight,
    key_value_weight,
    out_weight,
    router,
    expert_in,
    expert_out,
    score_weight,
):
    device = lax.axis_index("req")
    req_count = lax.axis_size("req")
    samples = tokens_new.shape[1]
    fresh_count = tokens_new.shape[2]
    model_width = tokens_new.shape[3]
    row_count = samples * fresh_count
    head_count = query_weight.shape[1] // HEAD_DIM
    kv_heads = key_value_weight.shape[2] // HEAD_DIM
    query_group_width = head_count // kv_heads
    pool_slots = slot_page_cache.shape[0]
    page_size = slot_page_cache.shape[1]
    slot_cap = max(1, pool_slots // req_count)
    score_scale = HEAD_DIM ** (-0.5)
    flat_tokens = tokens_new.reshape(row_count, model_width)
    normalized_input = rms_scale(flat_tokens, norm_gains[0]).astype(jnp.bfloat16)
    query_vectors = jnp.dot(
        normalized_input, query_weight, preferred_element_type=jnp.float32
    ).reshape(samples, fresh_count, head_count, HEAD_DIM)
    key_value_rows = jnp.dot(
        normalized_input,
        key_value_weight.reshape(model_width, 2 * kv_heads * HEAD_DIM),
        preferred_element_type=jnp.float32,
    ).reshape(samples, fresh_count, 2, kv_heads, HEAD_DIM)
    own_length = jnp.take(prefix_len, device)
    token_positions = (
        own_length + tail_len[0][:, None] + jnp.arange(fresh_count, dtype=jnp.int32)[None, :]
    )
    rotated_query = (
        apply_rotary(query_vectors, token_positions)
        .astype(jnp.bfloat16)
        .reshape(samples, fresh_count, kv_heads, query_group_width, HEAD_DIM)
    )
    key_rot = apply_rotary(key_value_rows[:, :, 0], token_positions).astype(jnp.bfloat16)
    value_new = key_value_rows[:, :, 1].astype(jnp.bfloat16)
    owner_homes = pool_home.reshape(req_count, pool_slots)
    owner_pages = pool_page.reshape(req_count, pool_slots)
    own_home = jnp.take(owner_homes, device, axis=0)
    slot_range = jnp.arange(pool_slots, dtype=jnp.int32)
    cap_range = jnp.arange(slot_cap, dtype=jnp.int32)
    same_home = own_home[:, None] == own_home[None, :]
    earlier = slot_range[:, None] <= slot_range[None, :]
    slot_rank = jnp.sum((same_home & earlier).astype(jnp.int32), axis=0)
    picked_slots = (
        own_home[None, None, :] == jnp.arange(req_count, dtype=jnp.int32)[:, None, None]
    ) & (slot_rank[None, None, :] == cap_range[None, :, None] + 1)
    slot_index = jnp.sum(
        picked_slots.astype(jnp.int32) * slot_range[None, None, :], axis=-1
    ).reshape(-1)
    page_range = jnp.arange(page_size, dtype=jnp.int32)
    outgoing = jnp.take(slot_page_cache, slot_index, axis=0).reshape(
        (req_count, slot_cap) + slot_page_cache.shape[1:]
    )
    arrived = lax.all_to_all(outgoing, "req", split_axis=0, concat_axis=0, tiled=True)
    home_match = owner_homes == device
    home_rank = jnp.cumsum(home_match.astype(jnp.int32), axis=1)
    wanted = home_match[:, None, :] & (home_rank[:, None, :] == cap_range[None, :, None] + 1)
    page_ids = jnp.where(
        jnp.any(wanted, axis=-1),
        jnp.sum(wanted.astype(jnp.int32) * owner_pages[:, None, :], axis=-1),
        -1,
    ).reshape(-1)
    blocks = arrived.reshape(req_count * slot_cap, page_size, 2, kv_heads, HEAD_DIM)
    page_scores = (
        jnp.einsum(
            "sikgd,btkd->bsikgt", rotated_query, blocks[:, :, 0], preferred_element_type=jnp.float32
        )
        * score_scale
    )
    page_spots = page_ids[:, None] * page_size + page_range[None, :]
    page_seen = ((page_spots < own_length) & (page_ids[:, None] >= 0))[:, None, None, None, None, :]
    page_top, page_total, page_weights = block_stats(page_scores, page_seen)
    page_numer = jnp.einsum(
        "bsikgt,btkd->bsikgd", page_weights, blocks[:, :, 1], preferred_element_type=jnp.float32
    )
    tail_count = tail_cache.shape[2]
    tail_block_list = tail_cache[0].reshape(
        samples, tail_count // page_size, page_size, 2, kv_heads, HEAD_DIM
    )
    tail_scores = (
        jnp.einsum(
            "sikgd,sbtkd->sbikgt",
            rotated_query,
            tail_block_list[:, :, :, 0],
            preferred_element_type=jnp.float32,
        )
        * score_scale
    )
    tail_spots = jnp.arange(tail_count, dtype=jnp.int32).reshape(tail_count // page_size, page_size)
    tail_seen = (tail_spots[None] < tail_len[0][:, None, None])[:, :, None, None, None, :]
    tail_top, tail_total, tail_weights = block_stats(tail_scores, tail_seen)
    tail_numer = jnp.einsum(
        "sbikgt,sbtkd->sbikgd",
        tail_weights,
        tail_block_list[:, :, :, 1],
        preferred_element_type=jnp.float32,
    )
    fresh_scores = (
        jnp.einsum("sikgd,sjkd->sikgj", rotated_query, key_rot, preferred_element_type=jnp.float32)
        * score_scale
    )
    fresh_range = jnp.arange(fresh_count, dtype=jnp.int32)
    fresh_seen = (fresh_range[None, :] <= fresh_range[:, None])[None, :, None, None, :]
    fresh_top, fresh_total, fresh_weights = block_stats(fresh_scores, fresh_seen)
    fresh_numer = jnp.einsum(
        "sikgj,sjkd->sikgd", fresh_weights, value_new, preferred_element_type=jnp.float32
    )
    overall = jnp.maximum(
        jnp.maximum(jnp.max(page_top, axis=0), jnp.max(tail_top, axis=1)), fresh_top
    )
    page_factor = jnp.exp(page_top - overall[None])
    tail_factor = jnp.exp(tail_top - overall[:, None])
    fresh_factor = jnp.exp(fresh_top - overall)
    denominator = (
        jnp.sum(page_factor * page_total, axis=0)
        + jnp.sum(tail_factor * tail_total, axis=1)
        + fresh_factor * fresh_total
    )
    numerator = (
        jnp.sum(page_factor[..., None] * page_numer, axis=0)
        + jnp.sum(tail_factor[..., None] * tail_numer, axis=1)
        + fresh_factor[..., None] * fresh_numer
    )
    attn_rows = (
        (numerator / denominator[..., None])
        .astype(jnp.bfloat16)
        .reshape(row_count, head_count * HEAD_DIM)
    )
    attn_part = jnp.dot(attn_rows, out_weight, preferred_element_type=jnp.float32)
    attn_out = lax.psum(attn_part, "tp")
    residual = (flat_tokens.astype(jnp.float32) + attn_out).astype(jnp.bfloat16)
    normed_moe = rms_scale(residual, norm_gains[1]).astype(jnp.bfloat16)
    logits = jnp.dot(normed_moe, router, preferred_element_type=jnp.float32)
    routing = routes.reshape(row_count, -1)
    top_count = routing.shape[1]
    expert_count = router.shape[1]
    expert_range = jnp.arange(expert_count, dtype=jnp.int32)
    route_table = (routing[:, :, None] == expert_range[None, None, :]).astype(jnp.float32)
    picked = jnp.sum(route_table * logits[:, None, :], axis=-1)
    gate_values = jax.nn.softmax(picked, axis=-1)
    local_experts = expert_in.shape[0]
    copies = local_experts * req_count // expert_count
    expert_slot = routing + expert_count * (device % copies)
    onehot = (routing.reshape(-1)[:, None] == expert_range[None, :]).astype(jnp.int32)
    arrival = jnp.sum(jnp.cumsum(onehot, axis=0) * onehot, axis=1) - 1
    target = (expert_slot.reshape(-1) * MOST + arrival).reshape(row_count, top_count)
    buffer = req_count * local_experts * MOST
    hits = (target[None, :, :] == jnp.arange(buffer, dtype=jnp.int32)[:, None, None]).astype(
        jnp.float32
    )
    spread = jnp.sum(hits, axis=-1).astype(jnp.bfloat16)
    combine = jnp.transpose(jnp.sum(hits * gate_values[None], axis=-1))
    outgoing_rows = (
        jnp.dot(spread, normed_moe, preferred_element_type=jnp.float32)
        .astype(jnp.bfloat16)
        .reshape(req_count, local_experts, MOST, model_width)
    )
    gate_up = jnp.einsum(
        "necd,edgf->necgf",
        lax.all_to_all(outgoing_rows, "req", split_axis=0, concat_axis=0, tiled=True),
        expert_in,
        preferred_element_type=jnp.float32,
    )
    hidden = (jax.nn.silu(gate_up[:, :, :, 0]) * gate_up[:, :, :, 1]).astype(jnp.bfloat16)
    result = jnp.einsum("necf,efd->necd", hidden, expert_out, preferred_element_type=jnp.float32)
    returned = lax.all_to_all(
        result.astype(jnp.bfloat16), "req", split_axis=0, concat_axis=0, tiled=True
    ).astype(result.dtype)
    mixed_part = jnp.dot(combine, returned.reshape(buffer, -1), precision=lax.Precision.HIGHEST)
    expert_mix = lax.psum(mixed_part.astype(jnp.bfloat16), "tp").astype(jnp.float32)
    layer_out = (residual.astype(jnp.float32) + expert_mix).astype(jnp.bfloat16)
    final_norm = rms_scale(layer_out, norm_gains[2])
    row_score = jnp.sum(final_norm * score_weight, axis=-1)
    return (
        layer_out.reshape(1, samples, fresh_count, model_width),
        row_score.reshape(1, samples, fresh_count),
    )


def solution(mesh):
    placed = (
        P("req", None, None, None),
        P(),
        P("req", None),
        P(),
        P(),
        P("req", None, None, "tp"),
        P("req", None, None, None, "tp"),
        P("req", None, None, None),
        P(),
        P(None, "tp"),
        P(None, None, "tp"),
        P("tp", None),
        P(),
        P("req", None, None, "tp"),
        P("req", "tp", None),
        P(),
    )
    return jax.shard_map(
        shards,
        mesh=mesh,
        in_specs=placed,
        out_specs=(P("req", None, None, None), P("req", None, None)),
        check_vma=False,
    )
```

profile of v0, /device:TPU:2, one launch (start us, length us, event | category | flops | bytes accessed | tf_op | source)
XLA Modules:
  0.0 399.7 jit_solution(14285597943707223789)
XLA Ops:
  7.2 0.9 reshape.516
  8.4 0.4 copy-done
  8.8 10.7 %gather_fusion = bf16[64,128,2,128]{3,2,1,0:T(2,128)(2,1)} fusion(bf16[32,128,2,128]{3,2,1,0:T(2,128)(2,1)S(1)} %copy-done, s32[1024]{0:T(1024)S(1)} %pad_clamp_fusion), kind=kCustom, calls=%fused_computation | custom fusion | bytes 8388864 | tf_op jit(solution)/shard_map/jit(_take)/gather | solution.py:110
  19.5 7.9 %fusion.4 = bf16[64,1,128,2,128]{4,3,2,1,0:T(2,128)(2,1)} fusion(bf16[64,128,2,128]{3,2,1,0:T(2,128)(2,1)} %gather_fusion, pred[64]{0:T(512)(128)(4,1)S(1)} %compare_and_fusion), kind=kLoop, calls=%fused_computation.9 | loop fusion | flops 2097152 | bytes 8388672 | tf_op jit(solution)/shard_map/jit(_take)/select_n | solution.py:110
  27.4 12.3 %all-to-all-start = ((bf16[64,1,128,2,128]{4,3,2,1,0:T(2,128)(2,1)}), bf16[64,1,128,2,128]{4,3,2,1,0:T(2,128)(2,1)}, u32[]{:S(2)}, u32[]{:S(2)}) async-start(bf16[64,1,128,2,128]{4,3,2,1,0:T(2,128)(2,1)} %fusion.4), calls=%async_computation | async-start | bytes 8388608 | tf_op jit(solution)/shard_map/all_to_all | solution.py:113
  39.7 0.2 all-reduce.3.cloned.1.call-start
  40.2 0.6 dynamic-slice.5
  40.8 0.2 copy.276
  41.4 11.1 %copy.280 = bf16[1,16,512,2,128]{2,4,3,1,0:T(8,128)(2,1)} copy(bf16[1,16,512,2,128]{4,3,2,1,0:T(2,128)(2,1)} %param.22) | data formatting | bytes 8388608 | tf_op args[6]
  52.6 6.9 %reshape_squeeze.3 = bf16[16,4,128,2,2,64]{2,1,5,4,3,0:T(4,128)(2,1)} reshape(bf16[1,16,512,2,128]{2,4,3,1,0:T(8,128)(2,1)} %copy.280) | data formatting | bytes 8388608 | tf_op jit(solution)/shard_map/reshape;squeeze | solution.py:136
  60.4 0.6 fusion.86
  61.3 0.3 fusion.47
  61.9 5.0 %fusion.85 = (bf16[16,4,128,1,2,64]{2,1,5,4,3,0:T(4,128)(2,1)S(1)}, bf16[16,4,128,1,2,64]{2,1,5,4,3,0:T(4,128)(2,1)}) fusion(bf16[16,4,128,2,2,64]{2,1,5,4,3,0:T(4,128)(2,1)} %reshape_squeeze.3), kind=kLoop, calls=%fused_computation.163 | loop fusion | bytes 8388608 | tf_op jit(solution)/shard_map/slice | solution.py:143
  67.0 0.6 fusion.31
  67.6 1.0 fusion.80
  68.6 0.7 copy.283
  69.4 0.2 copy.284
  69.6 0.3 fusion.45
  70.2 0.7 fusion.58
  71.1 0.7 fusion.83
  72.0 0.6 reduce-window.6
  73.5 62.3 %all-to-all-done = bf16[64,1,128,2,128]{4,3,2,1,0:T(2,128)(2,1)} async-done(((bf16[64,1,128,2,128]{4,3,2,1,0:T(2,128)(2,1)}), bf16[64,1,128,2,128]{4,3,2,1,0:T(2,128)(2,1)}, u32[]{:S(2)}, u32[]{:S(2)}) %all-to-all-start) | async-done | bytes 4194336 | tf_op jit(solution)/shard_map/all_to_all | solution.py:113
  135.8 10.9 %copy.272 = bf16[64,1,128,2,128]{2,4,3,0,1:T(8,128)(2,1)} copy(bf16[64,1,128,2,128]{4,3,2,1,0:T(2,128)(2,1)} %all-to-all-done) | data formatting | bytes 8388608 | tf_op jit(solution)/shard_map/all_to_all | solution.py:113
  146.8 3.1 fusion.6
  149.9 3.3 fusion.7
  153.3 0.3 multiply_reduce_fusion
  153.8 0.7 fusion.72
  154.5 11.1 %copy.345 = bf16[64,1,128,2,128]{2,4,0,3,1:T(8,128)(2,1)} copy(bf16[64,1,128,2,128]{4,3,2,1,0:T(2,128)(2,1)} %all-to-all-done) | data formatting | bytes 8388608 | tf_op jit(solution)/shard_map/reshape | solution.py:122
  165.7 3.0 fusion
  168.7 1.3 fusion.24
  170.2 0.9 fusion.87
  171.1 0.3 all-reduce.5.cloned.1.call-start
  171.4 42.5 %all-reduce.3.cloned.1.call-done = f32[32,1024]{1,0:T(8,128)} async-done(((f32[32,1024]{1,0:T(8,128)}), f32[32,1024]{1,0:T(8,128)}) %all-reduce.3.cloned.1.call-update) | async-done | bytes 131088 | tf_op jit(solution)/shard_map/psum | solution.py:189
  213.9 1.0 fusion.37
  215.7 0.6 convert_reduce_fusion
  216.3 1.8 convolution_convert_fusion
  218.0 2.4 reshape.522
  220.5 61.7 %all_to_all.15 = bf16[64,1,12,1024]{3,2,1,0:T(8,128)(2,1)S(1)} all-to-all(bf16[64,1,12,1024]{3,2,1,0:T(8,128)(2,1)S(1)} %bitcast.214), channel_id=1, replica_groups=mesh['req'=64,'tp'=4] {'req'}, dimensions={0} | all-to-all | bytes 3145728 | tf_op jit(solution)/shard_map/all_to_all | solution.py:219
  282.2 1.8 fusion.17
  284.0 0.6 fusion.16
  284.6 0.9 copy.321
  285.5 56.7 %all_to_all.16 = bf16[64,1,12,1024]{3,2,1,0:T(8,128)(2,1)} all-to-all(bf16[64,1,12,1024]{3,2,1,0:T(8,128)(2,1)S(1)} %copy.321), channel_id=1, replica_groups=mesh['req'=64,'tp'=4] {'req'}, dimensions={0} | all-to-all | bytes 3145728 | tf_op jit(solution)/shard_map/all_to_all | solution.py:225
  342.2 3.6 reshape.526
  345.9 2.9 convolution_convert_fusion.2
  348.8 41.5 %all-reduce.5.cloned.1.call-done = bf16[32,1024]{1,0:T(8,128)(2,1)} async-done(((bf16[32,1024]{1,0:T(8,128)(2,1)}), bf16[32,1024]{1,0:T(8,128)(2,1)}) %all-reduce.5.cloned.1.call-update) | async-done | bytes 65552 | tf_op jit(solution)/shard_map/psum | solution.py:229
  390.3 1.0 fusion.33
  391.2 0.7 reshape.527
  392.2 0.7 copy.322
  (109 shorter events, 5.1 us)
Async XLA Ops:
  7.2 1.6 copy-start
  27.4 12.6 %copy-start.12 = (s32[1,16,2,8]{1,3,2,0:T(8,128)S(1)}, s32[1,16,2,8]{1,3,2,0:T(8,128)}, u32[]{:S(2)}) copy-start(s32[1,16,2,8]{1,3,2,0:T(8,128)} %param.23) | copy-start | bytes 3076
  27.4 12.9 %copy-start.18 = (s32[64]{0:T(128)S(1)}, s32[64]{0:T(128)}, u32[]{:S(2)}) copy-start(s32[64]{0:T(128)} %param.17) | copy-start | bytes 772
  27.4 13.5 %copy-start.4 = (bf16[1024,256]{1,0:T(8,128)(2,1)S(1)}, bf16[1024,256]{1,0:T(8,128)(2,1)}, u32[]{:S(2)}) copy-start(bf16[1024,256]{1,0:T(8,128)(2,1)} %param.25) | copy-start | bytes 1572868
  27.4 13.9 %copy-start.8 = (s32[2048]{0:T(1024)S(1)}, s32[2048]{0:T(1024)}, u32[]{:S(2)}) copy-start(s32[2048]{0:T(1024)} %param.19) | copy-start | bytes 24580
  27.4 14.0 %copy-start.13 = (s32[2048]{0:T(1024)S(1)}, s32[2048]{0:T(1024)}, u32[]{:S(2)}) copy-start(s32[2048]{0:T(1024)} %param.20) | copy-start | bytes 24580
  27.4 108.5 %all-to-all-start = ((bf16[64,1,128,2,128]{4,3,2,1,0:T(2,128)(2,1)}), bf16[64,1,128,2,128]{4,3,2,1,0:T(2,128)(2,1)}, u32[]{:S(2)}, u32[]{:S(2)}) async-start(bf16[64,1,128,2,128]{4,3,2,1,0:T(2,128)(2,1)} %fusion.4), calls=%async_computation | async-start | bytes 8388608 | tf_op jit(solution)/shard_map/all_to_all | solution.py:113
  39.7 174.2 %all-reduce.3.cloned.1.call-start = ((), (), s32[]{:S(2)}) async-start(), calls=%async_computation.3 | async-start | bytes 262144 | tf_op jit(solution)/shard_map/psum | solution.py:189
  52.6 7.0 %copy-start.3 = (bf16[1,16,2,1024]{3,2,1,0:T(2,128)(2,1)S(1)}, bf16[1,16,2,1024]{3,2,1,0:T(2,128)(2,1)}, u32[]{:S(2)}) copy-start(bf16[1,16,2,1024]{3,2,1,0:T(2,128)(2,1)} %param.16) | copy-start | bytes 196612
  52.6 7.8 %copy-start.15 = (s32[1,16]{1,0:T(1,128)S(1)}, s32[1,16]{1,0:T(1,128)}, u32[]{:S(2)}) copy-start(s32[1,16]{1,0:T(1,128)} %param.18) | copy-start | bytes 196
  52.6 7.8 %copy-start.11 = (f32[3,1024]{1,0:T(4,128)S(1)}, f32[3,1024]{1,0:T(4,128)}, u32[]{:S(2)}) copy-start(f32[3,1024]{1,0:T(4,128)} %param.24) | copy-start | bytes 36868
  67.0 2.3 copy-start.5
  149.8 3.3 copy-start.10
  165.7 3.0 copy-start.2
  168.7 1.6 copy-start.6
  168.7 46.3 %copy-start.17 = (bf16[1024,32]{0,1:T(8,128)(2,1)S(1)}, bf16[1024,32]{0,1:T(8,128)(2,1)}, u32[]{:S(2)}) copy-start(bf16[1024,32]{0,1:T(8,128)(2,1)} %param.28) | copy-start | bytes 196612
  171.1 219.2 %all-reduce.5.cloned.1.call-start = ((), (), s32[]{:S(2)}) async-start(), calls=%async_computation.4 | async-start | bytes 131072 | tf_op jit(solution)/shard_map/psum | solution.py:229
  218.0 64.2 %copy-start.16 = (bf16[1,1024,2,128]{3,2,1,0:T(2,128)(2,1)S(1)}, bf16[1,1024,2,128]{3,2,1,0:T(2,128)(2,1)}, u32[]{:S(2)}) copy-start(bf16[1,1024,2,128]{3,2,1,0:T(2,128)(2,1)} %param.29) | copy-start | bytes 1572868
  220.5 63.5 %copy-start.7 = (bf16[1,128,1024]{2,1,0:T(8,128)(2,1)S(1)}, bf16[1,128,1024]{2,1,0:T(8,128)(2,1)}, u32[]{:S(2)}) copy-start(bf16[1,128,1024]{2,1,0:T(8,128)(2,1)} %param.30) | copy-start | bytes 786436
  285.5 107.3 %copy-start.1 = (bf16[32,128,2,128]{3,2,1,0:T(2,128)(2,1)S(1)}, bf16[32,128,2,128]{3,2,1,0:T(2,128)(2,1)}, u32[]{:S(2)}) copy-start(bf16[32,128,2,128]{3,2,1,0:T(2,128)(2,1)} %param.21) | copy-start | bytes 6291460
  342.2 49.7 %copy-start.9 = (f32[1,1024]{1,0:T(1,128)S(1)}, f32[1,1024]{1,0:T(1,128)}, u32[]{:S(2)}) copy-start(f32[1,1024]{1,0:T(1,128)} %get-tuple-element.70) | copy-start | bytes 12292
  342.2 49.7 %copy-start.14 = (f32[1024]{0:T(1024)S(1)}, f32[1024]{0:T(1024)}, u32[]{:S(2)}) copy-start(f32[1024]{0:T(1024)} %param.31) | copy-start | bytes 12292
Sparse Core Ops, SparseCore 0:
  171.2 42.6 all-reduce.2
  348.9 41.2 all-reduce.4
where the time goes:
time: 401 us; the launch traced here: 400 us
  waiting for transfers between devices  146 us (36%)
  blocking collectives  118 us (29%)
  local copies, waits for them, and re-layouts  69.6 us (17%)
  other arithmetic  19.8 us (5%)
  matrix products  17.5 us (4%)
  between operations  15.2 us (4%)
  starting transfers between devices  12.8 us (3%)
    all_to_all x1, waiting for transfers between devices, shards(): lax.all_to_all(outgoing, 'req', split_axis=0, concat_axis=0, tiled=True)  62.3 us
    all_to_all x1, blocking collectives, shards(): lax.all_to_all(outgoing_rows, 'req', split_axis=0, concat_axis=0, tiled=T...  61.7 us
    all_to_all x1, blocking collectives, shards(): lax.all_to_all(result.astype(jnp.bfloat16), 'req', split_axis=0, concat_a...  56.7 us
    psum x1, waiting for transfers between devices, shards(): attn_out = lax.psum(attn_part, 'tp')  42.5 us
    psum x1, waiting for transfers between devices, shards(): lax.psum(mixed_part.astype(jnp.bfloat16), 'tp').astype(jnp.float32)  41.5 us
    unnamed x43, local copies, waits for them, and re-layouts  12.7 us
    all_to_all x1, starting transfers between devices, shards(): lax.all_to_all(outgoing, 'req', split_axis=0, concat_axis=0, tiled=True)  12.3 us
    reshape x1, local copies, waits for them, and re-layouts, shards(): arrived.reshape(req_count * slot_cap, page_size, 2, kv_heads, HEAD_DIM)  11.1 us
  transfers between devices with their start and end apart: 3, of which 3 were waited for; matrix products, arithmetic and copies ran while one was open for 8% of the time, Pallas kernels for 0%

commit v1 on v0

--- a/solution.py
+++ b/solution.py
@@ -226,7 +226,9 @@
         result.astype(jnp.bfloat16), "req", split_axis=0, concat_axis=0, tiled=True
     ).astype(result.dtype)
     mixed_part = jnp.dot(combine, returned.reshape(buffer, -1), precision=lax.Precision.HIGHEST)
-    expert_mix = lax.psum(mixed_part.astype(jnp.bfloat16), "tp").astype(jnp.float32)
+    expert_mix = jnp.sum(lax.all_gather(mixed_part.astype(jnp.bfloat16), "tp"), axis=0).astype(
+        jnp.float32
+    )
     layer_out = (residual.astype(jnp.float32) + expert_mix).astype(jnp.bfloat16)
     final_norm = rms_scale(layer_out, norm_gains[2])
     row_score = jnp.sum(final_norm * score_weight, axis=-1)

time: 401 us -> 371 us (0.925)
  waiting for transfers between devices: 146 us -> 105 us
  blocking collectives: 118 us -> 131 us
    psum x1 -> x0, waiting for transfers between devices: 41.5 us -> none  [shards(): lax.psum(mixed_part.astype(jnp.bfloat16), 'tp').astype(jnp.float32)]
    all_gather x0 -> x1, blocking collectives: none -> 12.4 us  [shards(): lax.all_gather(mixed_part.astype(jnp.bfloat16), 'tp')]
  transfers between devices with their start and end apart: 3 -> 2, of which waited for: 3 -> 2; matrix products, arithmetic and copies ran while one was open for 8% -> 9% of each run, Pallas kernels for 0% -> 0%
where the time goes in v1:
time: 371 us; the launch traced here: 369 us
  blocking collectives  131 us (35%)
  waiting for transfers between devices  105 us (28%)
  local copies, waits for them, and re-layouts  69.7 us (19%)
  other arithmetic  19 us (5%)
  matrix products  16.9 us (5%)
  between operations  15.2 us (4%)
  starting transfers between devices  12.4 us (3%)
    all_to_all x1, waiting for transfers between devices, shards(): lax.all_to_all(outgoing, 'req', split_axis=0, concat_axis=0, tiled=True)  62.3 us
    all_to_all x1, blocking collectives, shards(): lax.all_to_all(outgoing_rows, 'req', split_axis=0, concat_axis=0, tiled=T...  62 us
    all_to_all x1, blocking collectives, shards(): lax.all_to_all(result.astype(jnp.bfloat16), 'req', split_axis=0, concat_a...  56.7 us
    psum x1, waiting for transfers between devices, shards(): attn_out = lax.psum(attn_part, 'tp')  42.8 us
    unnamed x43, local copies, waits for them, and re-layouts  12.8 us
    all_gather x1, blocking collectives, shards(): lax.all_gather(mixed_part.astype(jnp.bfloat16), 'tp')  12.4 us
    all_to_all x1, starting transfers between devices, shards(): lax.all_to_all(outgoing, 'req', split_axis=0, concat_axis=0, tiled=True)  12.3 us
    reshape x1, local copies, waits for them, and re-layouts, shards(): arrived.reshape(req_count * slot_cap, page_size, 2, kv_heads, HEAD_DIM)  11.1 us
  transfers between devices with their start and end apart: 2, of which 2 were waited for; matrix products, arithmetic and copies ran while one was open for 9% of the time, Pallas kernels for 0%

profile of v1, /device:TPU:2, one launch (start us, length us, event | category | flops | bytes accessed | tf_op | source)
XLA Modules:
  0.0 369.4 jit_solution(3850707497472056643)
XLA Ops:
  7.2 0.9 reshape.516
  8.4 0.4 copy-done
  8.8 10.7 %gather_fusion = bf16[64,128,2,128]{3,2,1,0:T(2,128)(2,1)} fusion(bf16[32,128,2,128]{3,2,1,0:T(2,128)(2,1)S(1)} %copy-done, s32[1024]{0:T(1024)S(1)} %pad_clamp_fusion), kind=kCustom, calls=%fused_computation | custom fusion | bytes 8388864 | tf_op jit(solution)/shard_map/jit(_take)/gather | solution.py:110
  19.5 7.9 %fusion.4 = bf16[64,1,128,2,128]{4,3,2,1,0:T(2,128)(2,1)} fusion(bf16[64,128,2,128]{3,2,1,0:T(2,128)(2,1)} %gather_fusion, pred[64]{0:T(512)(128)(4,1)S(1)} %compare_and_fusion), kind=kLoop, calls=%fused_computation.9 | loop fusion | flops 2097152 | bytes 8388672 | tf_op jit(solution)/shard_map/jit(_take)/select_n | solution.py:110
  27.4 12.3 %all-to-all-start = ((bf16[64,1,128,2,128]{4,3,2,1,0:T(2,128)(2,1)}), bf16[64,1,128,2,128]{4,3,2,1,0:T(2,128)(2,1)}, u32[]{:S(2)}, u32[]{:S(2)}) async-start(bf16[64,1,128,2,128]{4,3,2,1,0:T(2,128)(2,1)} %fusion.4), calls=%async_computation | async-start | bytes 8388608 | tf_op jit(solution)/shard_map/all_to_all | solution.py:113
  40.1 0.6 dynamic-slice.5
  40.7 0.2 copy.276
  41.3 11.3 %copy.280 = bf16[1,16,512,2,128]{2,4,3,1,0:T(8,128)(2,1)} copy(bf16[1,16,512,2,128]{4,3,2,1,0:T(2,128)(2,1)} %param.22) | data formatting | bytes 8388608 | tf_op args[6]
  52.5 6.9 %reshape_squeeze.3 = bf16[16,4,128,2,2,64]{2,1,5,4,3,0:T(4,128)(2,1)} reshape(bf16[1,16,512,2,128]{2,4,3,1,0:T(8,128)(2,1)} %copy.280) | data formatting | bytes 8388608 | tf_op jit(solution)/shard_map/reshape;squeeze | solution.py:136
  60.4 0.6 fusion.86
  61.3 0.3 fusion.47
  61.9 5.0 %fusion.85 = (bf16[16,4,128,1,2,64]{2,1,5,4,3,0:T(4,128)(2,1)S(1)}, bf16[16,4,128,1,2,64]{2,1,5,4,3,0:T(4,128)(2,1)}) fusion(bf16[16,4,128,2,2,64]{2,1,5,4,3,0:T(4,128)(2,1)} %reshape_squeeze.3), kind=kLoop, calls=%fused_computation.163 | loop fusion | bytes 8388608 | tf_op jit(solution)/shard_map/slice | solution.py:143
  66.9 0.6 fusion.31
  67.6 1.0 fusion.80
  68.5 0.7 copy.283
  69.3 0.2 copy.284
  69.5 0.3 fusion.45
  70.2 0.7 fusion.58
  71.1 0.7 fusion.83
  71.9 0.6 reduce-window.6
  73.5 62.3 %all-to-all-done = bf16[64,1,128,2,128]{4,3,2,1,0:T(2,128)(2,1)} async-done(((bf16[64,1,128,2,128]{4,3,2,1,0:T(2,128)(2,1)}), bf16[64,1,128,2,128]{4,3,2,1,0:T(2,128)(2,1)}, u32[]{:S(2)}, u32[]{:S(2)}) %all-to-all-start) | async-done | bytes 4194336 | tf_op jit(solution)/shard_map/all_to_all | solution.py:113
  135.8 10.9 %copy.272 = bf16[64,1,128,2,128]{2,4,3,0,1:T(8,128)(2,1)} copy(bf16[64,1,128,2,128]{4,3,2,1,0:T(2,128)(2,1)} %all-to-all-done) | data formatting | bytes 8388608 | tf_op jit(solution)/shard_map/all_to_all | solution.py:113
  146.8 3.1 fusion.6
  149.9 3.3 fusion.7
  153.3 0.3 multiply_reduce_fusion
  153.8 0.7 fusion.72
  154.5 11.1 %copy.345 = bf16[64,1,128,2,128]{2,4,0,3,1:T(8,128)(2,1)} copy(bf16[64,1,128,2,128]{4,3,2,1,0:T(2,128)(2,1)} %all-to-all-done) | data formatting | bytes 8388608 | tf_op jit(solution)/shard_map/reshape | solution.py:122
  165.7 3.0 fusion
  168.7 1.3 fusion.24
  170.2 0.9 fusion.87
  171.1 42.8 %all-reduce.2.cloned.1.call-done = f32[32,1024]{1,0:T(8,128)} async-done(((f32[32,1024]{1,0:T(8,128)}), f32[32,1024]{1,0:T(8,128)}) %all-reduce.2.cloned.1.call-update) | async-done | bytes 131088 | tf_op jit(solution)/shard_map/psum | solution.py:189
  213.9 1.0 fusion.37
  215.0 0.2 fusion.61
  215.2 0.2 select_reduce_fusion.1
  215.7 0.6 convert_reduce_fusion
  216.3 1.8 convolution_convert_fusion
  218.0 2.4 reshape.522
  220.5 62.0 %all_to_all.15 = bf16[64,1,12,1024]{3,2,1,0:T(8,128)(2,1)S(1)} all-to-all(bf16[64,1,12,1024]{3,2,1,0:T(8,128)(2,1)S(1)} %bitcast.215), channel_id=1, replica_groups=mesh['req'=64,'tp'=4] {'req'}, dimensions={0} | all-to-all | bytes 3145728 | tf_op jit(solution)/shard_map/all_to_all | solution.py:219
  282.4 1.8 fusion.17
  284.2 0.6 fusion.16
  284.8 0.9 copy.321
  285.7 56.7 %all_to_all.16 = bf16[64,1,12,1024]{3,2,1,0:T(8,128)(2,1)} all-to-all(bf16[64,1,12,1024]{3,2,1,0:T(8,128)(2,1)S(1)} %copy.321), channel_id=1, replica_groups=mesh['req'=64,'tp'=4] {'req'}, dimensions={0} | all-to-all | bytes 3145728 | tf_op jit(solution)/shard_map/all_to_all | solution.py:225
  342.5 3.6 reshape.526
  346.1 2.3 convolution_convert_fusion.2
  348.3 12.4 %all-gather = bf16[128,1024]{1,0:T(8,128)(2,1)S(1)} all-gather(bf16[32,1024]{1,0:T(8,128)(2,1)S(1)} %convolution_convert_fusion.2), channel_id=2, replica_groups=mesh['req'=64,'tp'=4] {'tp'}, dimensions={0}, use_global_device_ids=true | all-gather | bytes 327680 | tf_op jit(solution)/shard_map/all_gather | solution.py:229
  360.9 0.7 reshape.527
  361.6 0.2 fusion.36
  361.9 0.7 copy.322
  (108 shorter events, 4.7 us)
Async XLA Ops:
  7.2 1.6 copy-start
  27.4 12.4 %copy-start.12 = (s32[1,16,2,8]{1,3,2,0:T(8,128)S(1)}, s32[1,16,2,8]{1,3,2,0:T(8,128)}, u32[]{:S(2)}) copy-start(s32[1,16,2,8]{1,3,2,0:T(8,128)} %param.23) | copy-start | bytes 3076
  27.4 12.7 %copy-start.18 = (s32[64]{0:T(128)S(1)}, s32[64]{0:T(128)}, u32[]{:S(2)}) copy-start(s32[64]{0:T(128)} %param.17) | copy-start | bytes 772
  27.4 13.3 %copy-start.4 = (bf16[1024,256]{1,0:T(8,128)(2,1)S(1)}, bf16[1024,256]{1,0:T(8,128)(2,1)}, u32[]{:S(2)}) copy-start(bf16[1024,256]{1,0:T(8,128)(2,1)} %param.25) | copy-start | bytes 1572868
  27.4 13.7 %copy-start.8 = (s32[2048]{0:T(1024)S(1)}, s32[2048]{0:T(1024)}, u32[]{:S(2)}) copy-start(s32[2048]{0:T(1024)} %param.19) | copy-start | bytes 24580
  27.4 13.8 %copy-start.13 = (s32[2048]{0:T(1024)S(1)}, s32[2048]{0:T(1024)}, u32[]{:S(2)}) copy-start(s32[2048]{0:T(1024)} %param.20) | copy-start | bytes 24580
  27.4 108.5 %all-to-all-start = ((bf16[64,1,128,2,128]{4,3,2,1,0:T(2,128)(2,1)}), bf16[64,1,128,2,128]{4,3,2,1,0:T(2,128)(2,1)}, u32[]{:S(2)}, u32[]{:S(2)}) async-start(bf16[64,1,128,2,128]{4,3,2,1,0:T(2,128)(2,1)} %fusion.4), calls=%async_computation | async-start | bytes 8388608 | tf_op jit(solution)/shard_map/all_to_all | solution.py:113
  39.7 174.2 %all-reduce.2.cloned.1.call-start = ((), (), s32[]{:S(2)}) async-start(), calls=%async_computation.3 | async-start | bytes 262144 | tf_op jit(solution)/shard_map/psum | solution.py:189
  52.5 7.0 %copy-start.3 = (bf16[1,16,2,1024]{3,2,1,0:T(2,128)(2,1)S(1)}, bf16[1,16,2,1024]{3,2,1,0:T(2,128)(2,1)}, u32[]{:S(2)}) copy-start(bf16[1,16,2,1024]{3,2,1,0:T(2,128)(2,1)} %param.16) | copy-start | bytes 196612
  52.5 7.8 %copy-start.15 = (s32[1,16]{1,0:T(1,128)S(1)}, s32[1,16]{1,0:T(1,128)}, u32[]{:S(2)}) copy-start(s32[1,16]{1,0:T(1,128)} %param.18) | copy-start | bytes 196
  52.5 7.8 %copy-start.11 = (f32[3,1024]{1,0:T(4,128)S(1)}, f32[3,1024]{1,0:T(4,128)}, u32[]{:S(2)}) copy-start(f32[3,1024]{1,0:T(4,128)} %param.24) | copy-start | bytes 36868
  66.9 2.3 copy-start.5
  149.8 3.3 copy-start.10
  165.7 3.0 copy-start.2
  168.7 1.6 copy-start.6
  168.7 46.3 %copy-start.17 = (bf16[1024,32]{0,1:T(8,128)(2,1)S(1)}, bf16[1024,32]{0,1:T(8,128)(2,1)}, u32[]{:S(2)}) copy-start(bf16[1024,32]{0,1:T(8,128)(2,1)} %param.28) | copy-start | bytes 196612
  218.0 64.4 %copy-start.16 = (bf16[1,1024,2,128]{3,2,1,0:T(2,128)(2,1)S(1)}, bf16[1,1024,2,128]{3,2,1,0:T(2,128)(2,1)}, u32[]{:S(2)}) copy-start(bf16[1,1024,2,128]{3,2,1,0:T(2,128)(2,1)} %param.29) | copy-start | bytes 1572868
  220.5 63.8 %copy-start.7 = (bf16[1,128,1024]{2,1,0:T(8,128)(2,1)S(1)}, bf16[1,128,1024]{2,1,0:T(8,128)(2,1)}, u32[]{:S(2)}) copy-start(bf16[1,128,1024]{2,1,0:T(8,128)(2,1)} %param.30) | copy-start | bytes 786436
  285.7 76.8 %copy-start.1 = (bf16[32,128,2,128]{3,2,1,0:T(2,128)(2,1)S(1)}, bf16[32,128,2,128]{3,2,1,0:T(2,128)(2,1)}, u32[]{:S(2)}) copy-start(bf16[32,128,2,128]{3,2,1,0:T(2,128)(2,1)} %param.21) | copy-start | bytes 6291460
  342.5 19.1 %copy-start.9 = (f32[1,1024]{1,0:T(1,128)S(1)}, f32[1,1024]{1,0:T(1,128)}, u32[]{:S(2)}) copy-start(f32[1,1024]{1,0:T(1,128)} %get-tuple-element.70) | copy-start | bytes 12292
  342.5 19.1 %copy-start.14 = (f32[1024]{0:T(1024)S(1)}, f32[1024]{0:T(1024)}, u32[]{:S(2)}) copy-start(f32[1024]{0:T(1024)} %param.31) | copy-start | bytes 12292
Sparse Core Ops, SparseCore 0:
  171.2 42.6 all-reduce.1
